TPU v7x, 32 devices: a whole 2x2x4 slice. The times are simulated.
32 devices in a mesh: gx: 4 (over z), gy: 2 (over x), gz: 4 (over y, core).
Axes of the slice: x: 2, y: 2, z: 4, core: 2. Of those that a mesh axis runs over, the one named last changes fastest.
Arguments:
- element_state: float32 [9, 35, 4096], P(None, None, ('gx', 'gy', 'gz')), may hold values from -6 to 6
- jacobians: float32 [3, 9, 9, 4096], P(None, None, None, ('gx', 'gy', 'gz')), may hold values from -1.25 to 1.25
- stiffness: float32 [3, 35, 35], replicated, may hold values from -1 to 1
- projection: float32 [4, 15, 35], replicated, may hold values from -1 to 1
- flux_self: float32 [4, 9, 9, 4096], P(None, None, None, ('gx', 'gy', 'gz')), may hold values from -1 to 1
- flux_other: float32 [4, 9, 9, 4096], P(None, None, None, ('gx', 'gy', 'gz')), may hold values from -1 to 1
- face_source: int32 [4, 4096], P(None, ('gx', 'gy', 'gz')), may hold values from 0 to 607, as said below
- send_faces: int32 [6, 512], P(None, ('gx', 'gy', 'gz')), may hold values from 0 to 511
- cluster_mask: int32 [4096], P(('gx', 'gy', 'gz')), may hold values from 0 to 1
- seafloor_face: int32 [32768], P(('gx', 'gy', 'gz')), may hold values from -1 to 511, as said below
- ocean_cell: int32 [8, 4, 1024], P(('gx', 'gy')), may hold values from 0 to 65535
- ocean_weight: float32 [8, 4, 15, 1024], P(('gx', 'gy')), may hold values from 0 to 0.5
- height: float32 [1024, 512], P('gx', 'gy'), may hold values from -6 to 6
- east_flow: float32 [1024, 512], P('gx', 'gy'), may hold values from -6 to 6
- north_flow: float32 [1024, 512], P('gx', 'gy'), may hold values from -6 to 6
- water_depth: float32 [1024, 512], P('gx', 'gy'), may hold values from 0.5 to 2
Outputs:
- next_state: float32 [9, 35, 4096], P(None, None, ('gx', 'gy', 'gz'))
- new_height: float32 [1024, 512], P('gx', 'gy')
- new_east: float32 [1024, 512], P('gx', 'gy')
- new_north: float32 [1024, 512], P('gx', 'gy')
Inputs may be any that keep to these rules, and one draw needn't show every extreme that they name: `face_source`: within a partition, each of the 96 received columns (numbered from 512) is named by exactly one face; all other faces name the partition's own trace columns. `seafloor_face`: values are local face numbers or -1 for an empty slot. In each block of 128 slots of one partition for one tile the live slots come first and at least one is live; for one tile, the block of every partition is full.
All inputs are finite; a program needn't handle non-finite values.
Results may differ from a plain program's by a relative error of at most 0.0003.
Values sent between devices are 32-bit elements; how exact they have to be, the bound alone decides.
A program may use at most 128 MiB of HBM per device.

v0:
```python
import functools

import jax
import jax.numpy as jnp
from jax import lax
from jax.experimental import pallas as pl
from jax.experimental.pallas import tpu as pltpu
from jax.sharding import PartitionSpec as P

F32 = jnp.float32
BF16 = jnp.bfloat16
MESH = pl.DeviceIdType.MESH
time_step = 1.5
ocean_step = 0.5
NN = (((1,), (0,)), ((), ()))
NT = (((1,), (1,)), ((), ()))


def up(n, m):
    return -(-n // m) * m


def mm(a, b, dims=NN):
    return lax.dot_general(a, b, dims, preferred_element_type=F32)


def split(x):
    hi = x.astype(BF16)
    return hi, (x - hi.astype(F32)).astype(BF16)


def iota(shape, dim):
    return lax.broadcasted_iota(jnp.int32, shape, dim)


def ones_where(cond):
    return jnp.where(cond, 1.0, 0.0).astype(BF16)


def kernel(
    dims,
    state_ref,
    jac_ref,
    stiff_ref,
    proj_ref,
    self_ref,
    other_ref,
    source_ref,
    send_ref,
    mask_ref,
    floor_ref,
    cell_ref,
    weight_ref,
    height_ref,
    east_ref,
    north_ref,
    depth_ref,
    next_ref,
    new_height_ref,
    new_east_ref,
    new_north_ref,
    cur,
    integ,
    coup,
    lhs_d,
    lhs_v,
    lhs_p,
    lhs_t,
    table,
    numeric,
    floor_hot,
    face_hot,
    hot_c,
    w_out,
    w_in,
    v_out,
    v_in,
    faces_out,
    faces_in,
    flow_out,
    flow_in,
    rim_out,
    rim_in,
    w_send,
    w_recv,
    v_send,
    v_recv,
    f_send,
    f_recv,
    o_send,
    o_recv,
    r_send,
    r_recv,
):
    n_gx, n_gy, n_gz, nq, nb, nf, ne, slots, block = dims
    tiles = n_gx * n_gy
    devices = tiles * n_gz
    nbp, nfp = up(nb, 8), up(nf, 16)
    rows, cols = height_ref.shape
    i, j, k = lax.axis_index("gx"), lax.axis_index("gy"), lax.axis_index("gz")
    tile = i * n_gy + j
    me = tile * n_gz + k
    half = coup.shape[0]

    def place(n):
        return (n // (n_gy * n_gz), (n // n_gz) % n_gy, n % n_gz)

    barrier = pltpu.get_barrier_semaphore()

    @pl.loop(0, devices)
    def _(n):
        @pl.when(n != me)
        def _():
            pl.semaphore_signal(barrier, inc=1, device_id=place(n), device_id_type=MESH)

    tile_slots = tiles * slots
    group = min(tiles, 8)
    pieces = [slice(t * slots, (t + group) * slots) for t in range(0, tiles, group)]

    def in_row(layer, span):
        cells = cell_ref[0, pl.ds(layer, 1), span]
        return iota((rows, cells.shape[1]), 0) == cells // cols

    def in_col(layer, span):
        cells = cell_ref[0, pl.ds(layer, 1), span]
        return iota((cols, cells.shape[1]), 0) == cells % cols

    h_hi, h_lo = split(height_ref[...])
    for number, piece in enumerate(pieces):
        hot = ones_where(in_col(k, piece))
        picked = mm(h_hi, hot) + mm(h_lo, hot)
        heights = jnp.sum(jnp.where(in_row(k, piece), picked, 0.0), axis=0, keepdims=True)
        for part in range(group):
            t = number * group + part
            span = slice(t * slots, (t + 1) * slots)
            w_out[t, 0:nf, :] = weight_ref[0, k, :, span]
            w_out[t, nf : nf + 1, :] = heights[:, part * slots : (part + 1) * slots]

    square = iota((rows, cols), 0) == iota((rows, cols), 1)

    def as_row(column):
        return jnp.sum(jnp.where(square, column, 0.0), axis=0, keepdims=True)

    def as_column(row):
        return jnp.sum(jnp.where(square, row, 0.0), axis=1, keepdims=True)

    flow_out[0] = east_ref[0:1, :]
    flow_out[1] = east_ref[rows - 1 : rows, :]
    flow_out[2] = as_row(north_ref[:, 0:1])
    flow_out[3] = as_row(north_ref[:, cols - 1 : cols])

    pl.semaphore_wait(barrier, devices - 1)

    there = (i > 0, i < n_gx - 1, j > 0, j < n_gy - 1, k > 0, k < n_gz - 1)
    who = ((i - 1, j, k), (i + 1, j, k), (i, j - 1, k), (i, j + 1, k), (i, j, k - 1), (i, j, k + 1))

    def exchange(out, into, send, recv, direction):
        return pltpu.make_async_remote_copy(
            src_ref=out.at[direction],
            dst_ref=into.at[direction ^ 1],
            send_sem=send.at[direction],
            recv_sem=recv.at[direction ^ 1],
            device_id=who[direction],
            device_id_type=MESH,
        )

    def start_exchange(out, into, send, recv, count):
        for direction in range(count):

            @pl.when(there[direction])
            def _():
                exchange(out, into, send, recv, direction).start()

            @pl.when(jnp.logical_not(there[direction]))
            def _():
                into[direction] = jnp.zeros(into.shape[1:], F32)

    def end_exchange(out, into, send, recv, count):
        for direction in range(count):

            @pl.when(there[direction])
            def _():
                exchange(out, into, send, recv, direction).wait_send()
                pltpu.make_async_remote_copy(
                    src_ref=out.at[direction],
                    dst_ref=into.at[direction],
                    send_sem=send.at[direction],
                    recv_sem=recv.at[direction],
                    device_id=who[direction],
                    device_id_type=MESH,
                ).wait_recv()

    def weights_to(t, slot):
        return pltpu.make_async_remote_copy(
            src_ref=w_out.at[t],
            dst_ref=w_in.at[slot],
            send_sem=w_send.at[t],
            recv_sem=w_recv.at[slot],
            device_id=(t // n_gy, t % n_gy, k),
            device_id_type=MESH,
        )

    @pl.loop(0, tiles)
    def _(t):
        @pl.when(t != tile)
        def _():
            weights_to(t, tile).start()

    start_exchange(flow_out, flow_in, o_send, o_recv, 4)
    w_in[tile] = w_out[tile]

    for ref in (lhs_d, lhs_v, lhs_p, lhs_t, coup, cur, integ):
        ref[...] = jnp.zeros(ref.shape, ref.dtype)
    eye_b = ones_where(iota((nbp, nb), 0) == iota((nbp, nb), 1))

    def spots(count, width, first, second):
        r, c = iota((count, width), 0), iota((count, width), 1)
        once = c == first + r
        return ones_where(once | (c == second + r)), ones_where(once)

    total_d = jnp.zeros((nbp, 2 * half), F32)
    total_dl, total_v, total_vl = total_d, total_d, total_d
    for d in range(3):
        both, once = spots(nb, 2 * half, d * nbp, half + d * nbp)
        s_hi, s_lo = split(stiff_ref[d])
        total_d += mm(mm(eye_b, s_hi).astype(BF16), both)
        total_dl += mm(mm(eye_b, s_lo).astype(BF16), once)
        total_v += mm(mm(eye_b, s_hi, NT).astype(BF16), both)
        total_vl += mm(mm(eye_b, s_lo, NT).astype(BF16), once)
    lhs_d[0:nbp, :] = -total_d
    lhs_d[nbp : 2 * nbp, :] = -total_dl
    lhs_v[0:nbp, :] = total_v
    lhs_v[nbp : 2 * nbp, :] = total_vl

    nbk = integ.shape[0]
    faces = 4 * nfp
    both_b, once_b = spots(nb, 2 * nbk, 0, nbk)
    total_t = jnp.zeros((nbp, 2 * faces), F32)
    total_tl = total_t
    for f in range(4):
        both, once = spots(nf, 2 * faces, f * nfp, faces + f * nfp)
        p_hi, p_lo = split(proj_ref[f])
        lhs_p[f * nfp : f * nfp + nf, :] = mm(p_hi, both_b)
        lhs_p[faces + f * nfp : faces + f * nfp + nf, :] = mm(p_lo, once_b)
        total_t += mm(mm(eye_b, p_hi, NT).astype(BF16), both)
        total_tl += mm(mm(eye_b, p_lo, NT).astype(BF16), once)
    lhs_t[0:nbp, :] = total_t
    lhs_t[nbp : 2 * nbp, :] = total_tl

    def halves(lhs, rhs):
        hi, lo = split(rhs)
        out = mm(lhs[...].astype(BF16), jnp.concatenate([hi, lo], axis=0))
        count = out.shape[0] // 2
        return out[:count] + out[count:]

    for q in range(nq):
        cur[0:nb, q * ne : (q + 1) * ne] = state_ref[q]
    integ[0:nbp, :] = time_step * cur[...]

    def couple(values):
        @pl.loop(0, nq)
        def _(p):
            lane = pl.ds(pl.multiple_of(p * ne, ne), ne)
            sums = [None] * 3
            for q in range(nq):
                value = values[0:nbp, q * ne : (q + 1) * ne]
                for d in range(3):
                    term = jac_ref[d, p, q : q + 1, :] * value
                    sums[d] = term if q == 0 else sums[d] + term
            for d in range(3):
                coup[d * nbp : (d + 1) * nbp, lane] = sums[d]

    weight_now = time_step
    for degree in range(1, 5):
        couple(cur)
        weight_now = weight_now * time_step / (degree + 1)
        moved = halves(lhs_d, coup[...])
        if degree < 4:
            cur[...] = moved
        integ[0:nbp, :] += weight_now * moved

    traces = halves(lhs_p, integ[...])
    for q in range(nq):
        for f in range(4):
            table[q * nfp : (q + 1) * nfp, f * ne : (f + 1) * ne] = traces[
                f * nfp : (f + 1) * nfp, q * ne : (q + 1) * ne
            ]
    t_hi, t_lo = split(table[...])

    sends = 6 * block
    pick = ones_where(iota((sends, 6), 0) // block == iota((sends, 6), 1))
    index = send_ref[...]
    high = mm(pick, (index // 16).astype(F32).astype(BF16))
    low = mm(pick, (index % 16).astype(F32).astype(BF16))
    which = iota((sends, block), 0) % block == iota((sends, block), 1)
    chosen = jnp.sum(jnp.where(which, high * 16.0 + low, 0.0), axis=1, keepdims=True)
    send_hot = ones_where(iota((sends, 4 * ne), 1) == chosen.astype(jnp.int32))
    outgoing = mm(send_hot, t_hi, NT) + mm(send_hot, t_lo, NT)
    for direction in range(6):
        faces_out[direction] = outgoing[direction * block : (direction + 1) * block, :]
    start_exchange(faces_out, faces_in, f_send, f_recv, 6)

    for piece in pieces:
        floors = floor_ref[:, piece]
        floor_hot[:, piece] = ones_where(iota((4 * ne, floors.shape[1]), 0) == floors)
    vertical = slice((nq - 1) * nfp, nq * nfp)
    uptrace = mm(t_hi[vertical], floor_hot[...]) + mm(t_lo[vertical], floor_hot[...])

    @pl.loop(0, tiles)
    def _(t):
        @pl.when(t != tile)
        def _():
            weights_to(t, t).wait()

    for t in range(tiles):
        v_out[t] = jnp.sum(
            w_in[t, 0:nf, :] * uptrace[0:nf, t * slots : (t + 1) * slots], axis=0, keepdims=True
        )

    def values_to(n, slot):
        return pltpu.make_async_remote_copy(
            src_ref=v_out.at[n // n_gz],
            dst_ref=v_in.at[slot],
            send_sem=v_send.at[n],
            recv_sem=v_recv.at[slot],
            device_id=place(n),
            device_id_type=MESH,
        )

    mine = k * tiles + tile

    @pl.loop(0, devices)
    def _(n):
        @pl.when(n != me)
        def _():
            values_to(n, mine).start()

    v_in[mine] = v_out[tile]

    @pl.loop(0, n_gz)
    def _(layer):
        for span in pieces:
            hot_c[layer, :, span] = ones_where(in_col(layer, span))

    couple(integ)
    volume = halves(lhs_v, coup[...])

    @pl.loop(0, nq)
    def _(p):
        lane = pl.ds(pl.multiple_of(p * ne, ne), ne)
        for f in range(4):
            total = None
            for q in range(nq):
                own = table[q * nfp : (q + 1) * nfp, f * ne : (f + 1) * ne]
                term = self_ref[f, q, pl.ds(p, 1), :] * own
                total = term if q == 0 else total + term
            numeric[f * nfp : (f + 1) * nfp, lane] = total

    loads = jnp.concatenate(
        [w_in[t] * w_in[t, nf : nf + 1, :] for t in range(tiles)], axis=1
    )
    l_hi, l_lo = split(loads)
    face_load = mm(l_hi, floor_hot[...], NT) + mm(l_lo, floor_hot[...], NT)
    for f in range(4):
        numeric[f * nfp : f * nfp + nf, 2 * ne : 3 * ne] += face_load[
            0:nf, f * ne : (f + 1) * ne
        ]

    for f in range(4):
        face_hot[:, f * ne : (f + 1) * ne] = ones_where(
            iota((face_hot.shape[0], ne), 0) == source_ref[f : f + 1, :]
        )
    hot_own = face_hot[0 : 4 * ne, :]
    remote = mm(t_hi, hot_own) + mm(t_lo, hot_own)
    end_exchange(faces_out, faces_in, f_send, f_recv, 6)
    arrived = jnp.concatenate([faces_in[direction] for direction in range(6)], axis=0)
    a_hi, a_lo = split(arrived)
    width = nq * nfp
    eye_t = ones_where(iota((width, width), 0) == iota((width, width), 1))
    hot_far = face_hot[4 * ne : 4 * ne + sends, :]
    remote = remote + mm(mm(eye_t, a_hi, NT).astype(BF16), hot_far)
    remote = remote + mm(mm(eye_t, a_lo, NT).astype(BF16), hot_far)
    table[...] = remote

    @pl.loop(0, nq)
    def _(p):
        lane = pl.ds(pl.multiple_of(p * ne, ne), ne)
        for f in range(4):
            total = numeric[f * nfp : (f + 1) * nfp, lane]
            for q in range(nq):
                far = table[q * nfp : (q + 1) * nfp, f * ne : (f + 1) * ne]
                total = total + other_ref[f, q, pl.ds(p, 1), :] * far
            numeric[f * nfp : (f + 1) * nfp, lane] = total

    change = volume - halves(lhs_t, numeric[...])
    finest = mask_ref[...] > 0
    for q in range(nq):
        state = state_ref[q]
        next_ref[q] = jnp.where(finest, state + change[0:nb, q * ne : (q + 1) * ne], state)

    end_exchange(flow_out, flow_in, o_send, o_recv, 4)
    first_row, last_row = iota((rows, cols), 0) == 0, iota((rows, cols), 0) == rows - 1
    first_col, last_col = iota((rows, cols), 1) == 0, iota((rows, cols), 1) == cols - 1

    def slope_x(grid, rim):
        before = jnp.where(first_row, rim[0], pltpu.roll(grid, 1, 0))
        after = jnp.where(last_row, rim[1], pltpu.roll(grid, rows - 1, 0))
        return (after - before) * 0.5

    def slope_y(grid, rim):
        before = jnp.where(first_col, as_column(rim[2]), pltpu.roll(grid, 1, 1))
        after = jnp.where(last_col, as_column(rim[3]), pltpu.roll(grid, cols - 1, 1))
        return (after - before) * 0.5

    slopes = slope_x(east_ref[...], flow_in) + slope_y(north_ref[...], flow_in)
    base = height_ref[...] - ocean_step * (depth_ref[...] * slopes)

    @pl.loop(0, devices)
    def _(n):
        @pl.when(n != me)
        def _():
            values_to(n, (n % n_gz) * tiles + n // n_gz).wait()

    source = jnp.zeros((rows, cols), F32)
    for layer in range(n_gz):
        for number, piece in enumerate(pieces):
            first = layer * tiles + number * group
            values = jnp.concatenate([v_in[first + part] for part in range(group)], axis=1)
            v_hi, v_lo = split(values)
            here, other = in_row(layer, piece), hot_c[layer, :, piece]
            for part in (v_hi, v_lo):
                spread = jnp.where(here, part.astype(F32), 0.0).astype(BF16)
                source += mm(spread, other, NT)
    new_height = base + ocean_step * source
    rim_out[0] = new_height[0:1, :]
    rim_out[1] = new_height[rows - 1 : rows, :]
    rim_out[2] = as_row(new_height[:, 0:1])
    rim_out[3] = as_row(new_height[:, cols - 1 : cols])
    start_exchange(rim_out, rim_in, r_send, r_recv, 4)
    new_height_ref[...] = new_height
    end_exchange(rim_out, rim_in, r_send, r_recv, 4)
    new_east_ref[...] = east_ref[...] - ocean_step * slope_x(new_height, rim_in)
    new_north_ref[...] = north_ref[...] - ocean_step * slope_y(new_height, rim_in)


def on_device(
    sizes,
    element_state,
    jacobians,
    stiffness,
    projection,
    flux_self,
    flux_other,
    face_source,
    send_faces,
    cluster_mask,
    seafloor_face,
    ocean_cell,
    ocean_weight,
    height,
    east_flow,
    north_flow,
    water_depth,
):
    n_gx, n_gy, n_gz = sizes
    nq, nb, ne = element_state.shape
    nf = projection.shape[1]
    tiles = n_gx * n_gy
    devices = tiles * n_gz
    slots = seafloor_face.shape[0] // tiles
    block = send_faces.shape[1]
    rows, cols = height.shape
    nbp, nfp = up(nb, 8), up(nf, 16)
    half = up(3 * nbp, 16)
    nbk = up(nb, 16)
    faces = 4 * nfp
    args = (
        element_state,
        jacobians,
        stiffness,
        projection,
        flux_self,
        flux_other,
        face_source,
        send_faces,
        cluster_mask.reshape(1, -1),
        seafloor_face.reshape(1, -1),
        ocean_cell,
        ocean_weight,
        height,
        east_flow,
        north_flow,
        water_depth,
    )
    scratch = [
        pltpu.VMEM((nbp, nq * ne), F32),
        pltpu.VMEM((nbk, nq * ne), F32),
        pltpu.VMEM((half, nq * ne), F32),
        pltpu.VMEM((2 * nbp, 2 * half), F32),
        pltpu.VMEM((2 * nbp, 2 * half), F32),
        pltpu.VMEM((2 * faces, 2 * nbk), F32),
        pltpu.VMEM((2 * nbp, 2 * faces), F32),
        pltpu.VMEM((nq * nfp, 4 * ne), F32),
        pltpu.VMEM((faces, nq * ne), F32),
        pltpu.VMEM((4 * ne, tiles * slots), BF16),
        pltpu.VMEM((up(4 * ne + 6 * block, 16), 4 * ne), BF16),
        pltpu.VMEM((n_gz, cols, tiles * slots), BF16),
        pltpu.VMEM((tiles, nfp, slots), F32),
        pltpu.VMEM((tiles, nfp, slots), F32),
        pltpu.VMEM((tiles, 1, slots), F32),
        pltpu.VMEM((devices, 1, slots), F32),
        pltpu.VMEM((6, block, nq * nfp), F32),
        pltpu.VMEM((6, block, nq * nfp), F32),
        pltpu.VMEM((4, 1, cols), F32),
        pltpu.VMEM((4, 1, cols), F32),
        pltpu.VMEM((4, 1, cols), F32),
        pltpu.VMEM((4, 1, cols), F32),
    ]
    for count in (tiles, devices, 6, 4, 4):
        scratch += [pltpu.SemaphoreType.DMA((count,)), pltpu.SemaphoreType.DMA((count,))]
    return pl.pallas_call(
        functools.partial(kernel, (n_gx, n_gy, n_gz, nq, nb, nf, ne, slots, block)),
        out_shape=(
            jax.ShapeDtypeStruct(element_state.shape, F32),
            jax.ShapeDtypeStruct(height.shape, F32),
            jax.ShapeDtypeStruct(height.shape, F32),
            jax.ShapeDtypeStruct(height.shape, F32),
        ),
        in_specs=[pl.BlockSpec(memory_space=pltpu.VMEM)] * len(args),
        out_specs=[pl.BlockSpec(memory_space=pltpu.VMEM)] * 4,
        scratch_shapes=scratch,
        compiler_params=pltpu.CompilerParams(collective_id=0, has_side_effects=True),
        name="step",
    )(*args)


def solution(mesh):
    sizes = tuple(mesh.shape[axis] for axis in ("gx", "gy", "gz"))
    return jax.shard_map(
        functools.partial(on_device, sizes),
        mesh=mesh,
        in_specs=(
            P(None, None, ("gx", "gy", "gz")),
            P(None, None, None, ("gx", "gy", "gz")),
            P(),
            P(),
            P(None, None, None, ("gx", "gy", "gz")),
            P(None, None, None, ("gx", "gy", "gz")),
            P(None, ("gx", "gy", "gz")),
            P(None, ("gx", "gy", "gz")),
            P(("gx", "gy", "gz")),
            P(("gx", "gy", "gz")),
            P(("gx", "gy"), None, None),
            P(("gx", "gy"), None, None, None),
            P("gx", "gy"),
            P("gx", "gy"),
            P("gx", "gy"),
            P("gx", "gy"),
        ),
        out_specs=(P(None, None, ("gx", "gy", "gz")), P("gx", "gy"), P("gx", "gy"), P("gx", "gy")),
        check_vma=False,
    )
```

profile of v0, /device:TPU:0, one launch (start us, length us, event | category | flops | bytes accessed | tf_op | source)
XLA Modules:
  0.0 36.3 jit_solution(2733590319275357094)
XLA Ops:
  0.6 0.0 copy-start.3
  0.6 1.4 %copy.21.proj_ref = f32[4,15,35]{2,1,0:T(8,128)} copy(f32[4,15,35]{2,0,1:T(4,128)} %param.19) | data formatting | bytes 16800 | tf_op args[3]
  2.1 1.6 %copy.20.jac_ref = f32[3,9,9,128]{3,2,1,0:T(8,128)} copy(f32[3,9,9,128]{3,0,2,1:T(4,128)} %param.17) | data formatting | bytes 248832 | tf_op args[1]
  3.7 0.0 copy-done.3
  3.7 0.0 copy-start.4
  3.7 0.8 %copy.24.weight_ref = f32[1,4,15,1024]{3,2,1,0:T(8,128)} copy(f32[1,4,15,1024]{3,1,2,0:T(4,128)S(1)} %copy-done.3) | data formatting | bytes 491520 | tf_op args[11]
  4.5 0.1 copy-done.4
  4.6 0.0 copy-start.5
  4.6 0.7 %copy.22.self_ref = f32[4,9,9,128]{3,2,1,0:T(8,128)} copy(f32[4,9,9,128]{3,0,2,1:T(4,128)S(1)} %copy-done.4) | data formatting | bytes 331776 | tf_op args[4]
  5.3 0.3 copy-done.5
  5.6 0.7 %copy.23.other_ref = f32[4,9,9,128]{3,2,1,0:T(8,128)} copy(f32[4,9,9,128]{3,0,2,1:T(4,128)S(1)} %copy-done.5) | data formatting | bytes 331776 | tf_op args[5]
  6.3 25.6 %step.1 = (f32[9,35,128]{2,1,0:T(8,128)}, f32[256,256]{1,0:T(8,128)}, f32[256,256]{1,0:T(8,128)}, f32[256,256]{1,0:T(8,128)}) custom-call(f32[9,35,128]{2,1,0:T(8,128)} %state_ref.1, f32[3,9,9,128]{3,2,1,0:T(8,128)} %copy.20.jac_ref, f32[3,35,35]{2,1,0:T(8,128)} %stiff_ref.1, f32[4,15,35]{2,1,0:T(8,128)} %copy.21.proj_ref, f32[4,9,9,128]{3,2,1,0:T(8,128)} %copy.22.self_ref, ...), custom_call_target="tpu_custom_call" | custom-call | tf_op jit(solution)/shard_map/step/pallas_call | solution.py:521
  31.9 0.0 copy-start.2
  31.9 1.6 %copy.29 = f32[9,35,128]{2,1,0:T(8,128)} copy(f32[9,35,128]{2,1,0:T(8,128)} %get-tuple-element.8) | data formatting | bytes 322560
  33.6 0.0 copy-done.2
  33.6 0.0 copy-start.1
  33.6 0.7 %copy.30 = f32[256,256]{1,0:T(8,128)} copy(f32[256,256]{1,0:T(8,128)S(1)} %copy-done.2) | data formatting | bytes 524288
  34.3 0.3 copy-done.1
  34.6 0.0 copy-start
  34.6 0.7 %copy.31 = f32[256,256]{1,0:T(8,128)} copy(f32[256,256]{1,0:T(8,128)S(1)} %copy-done.1) | data formatting | bytes 524288
  35.3 0.3 copy-done
  35.6 0.7 %copy.32 = f32[256,256]{1,0:T(8,128)} copy(f32[256,256]{1,0:T(8,128)S(1)} %copy-done) | data formatting | bytes 524288
Async XLA Ops:
  0.6 3.0 %copy-start.3 = (f32[1,4,15,1024]{3,1,2,0:T(4,128)S(1)}, f32[1,4,15,1024]{3,1,2,0:T(4,128)}, u32[]{:S(2)}) copy-start(f32[1,4,15,1024]{3,1,2,0:T(4,128)} %param.27) | copy-start | bytes 737284
  3.7 0.9 %copy-start.4 = (f32[4,9,9,128]{3,0,2,1:T(4,128)S(1)}, f32[4,9,9,128]{3,0,2,1:T(4,128)}, u32[]{:S(2)}) copy-start(f32[4,9,9,128]{3,0,2,1:T(4,128)} %param.20) | copy-start | bytes 497668
  4.6 1.0 %copy-start.5 = (f32[4,9,9,128]{3,0,2,1:T(4,128)S(1)}, f32[4,9,9,128]{3,0,2,1:T(4,128)}, u32[]{:S(2)}) copy-start(f32[4,9,9,128]{3,0,2,1:T(4,128)} %param.21) | copy-start | bytes 497668
  31.9 1.7 %copy-start.2 = (f32[256,256]{1,0:T(8,128)S(1)}, f32[256,256]{1,0:T(8,128)}, u32[]{:S(2)}) copy-start(f32[256,256]{1,0:T(8,128)} %get-tuple-element.9) | copy-start | bytes 786436
  33.6 1.0 %copy-start.1 = (f32[256,256]{1,0:T(8,128)S(1)}, f32[256,256]{1,0:T(8,128)}, u32[]{:S(2)}) copy-start(f32[256,256]{1,0:T(8,128)} %get-tuple-element.10) | copy-start | bytes 786436
  34.6 1.0 %copy-start = (f32[256,256]{1,0:T(8,128)S(1)}, f32[256,256]{1,0:T(8,128)}, u32[]{:S(2)}) copy-start(f32[256,256]{1,0:T(8,128)} %get-tuple-element.11) | copy-start | bytes 786436
where the time goes:
time: 36.7 us; the launch traced here: 36.3 us
  Pallas kernels  25.6 us (70%)
  local copies, waits for them, and re-layouts  10.1 us (28%)
  between operations  0.66 us (2%)
    pallas_call x1, Pallas kernels, on_device(): pl.pallas_call(functools.partial(kernel, (n_gx, n_gy, n_gz, nq, nb, nf, n...  25.6 us
    unnamed x21, local copies, waits for them, and re-layouts  10.1 us

commit v1 on v0

--- a/solution.py
+++ b/solution.py
@@ -37,28 +37,48 @@
     return jnp.where(cond, 1.0, 0.0).astype(BF16)
 
 
+def slopers(rows, cols):
+    square = iota((rows, cols), 0) == iota((rows, cols), 1)
+
+    def as_column(row):
+        return jnp.sum(jnp.where(square, row, 0.0), axis=1, keepdims=True)
+
+    first_row, last_row = iota((rows, cols), 0) == 0, iota((rows, cols), 0) == rows - 1
+    first_col, last_col = iota((rows, cols), 1) == 0, iota((rows, cols), 1) == cols - 1
+
+    def slope_x(grid, rim):
+        before = jnp.where(first_row, rim[0], pltpu.roll(grid, 1, 0))
+        after = jnp.where(last_row, rim[1], pltpu.roll(grid, rows - 1, 0))
+        return (after - before) * 0.5
+
+    def slope_y(grid, rim):
+        before = jnp.where(first_col, as_column(rim[2]), pltpu.roll(grid, 1, 1))
+        after = jnp.where(last_col, as_column(rim[3]), pltpu.roll(grid, cols - 1, 1))
+        return (after - before) * 0.5
+
+    return slope_x, slope_y
+
+
 def kernel(
     dims,
     state_ref,
     jac_ref,
     stiff_ref,
     proj_ref,
-    self_ref,
-    other_ref,
+    self_hbm,
+    other_hbm,
     source_ref,
     send_ref,
-    mask_ref,
     floor_ref,
     cell_ref,
     weight_ref,
-    height_ref,
-    east_ref,
-    north_ref,
-    depth_ref,
-    next_ref,
+    height_hbm,
+    east_hbm,
+    north_hbm,
+    depth_hbm,
+    change_ref,
     new_height_ref,
-    new_east_ref,
-    new_north_ref,
+    rim_ref,
     cur,
     integ,
     coup,
@@ -91,6 +111,13 @@
     o_recv,
     r_send,
     r_recv,
+    self_ref,
+    other_ref,
+    height_ref,
+    east_ref,
+    north_ref,
+    depth_ref,
+    in_sem,
 ):
     n_gx, n_gy, n_gz, nq, nb, nf, ne, slots, block = dims
     tiles = n_gx * n_gy
@@ -113,6 +140,22 @@
         def _():
             pl.semaphore_signal(barrier, inc=1, device_id=place(n), device_id_type=MESH)
 
+    loads_in = [
+        pltpu.make_async_copy(source, target, in_sem.at[number])
+        for number, (source, target) in enumerate(
+            (
+                (height_hbm, height_ref),
+                (east_hbm, east_ref),
+                (north_hbm, north_ref),
+                (self_hbm, self_ref),
+                (depth_hbm, depth_ref),
+                (other_hbm, other_ref),
+            )
+        )
+    ]
+    for load in loads_in:
+        load.start()
+
     tile_slots = tiles * slots
     group = min(tiles, 8)
     pieces = [slice(t * slots, (t + group) * slots) for t in range(0, tiles, group)]
@@ -125,31 +168,10 @@
         cells = cell_ref[0, pl.ds(layer, 1), span]
         return iota((cols, cells.shape[1]), 0) == cells % cols
 
-    h_hi, h_lo = split(height_ref[...])
-    for number, piece in enumerate(pieces):
-        hot = ones_where(in_col(k, piece))
-        picked = mm(h_hi, hot) + mm(h_lo, hot)
-        heights = jnp.sum(jnp.where(in_row(k, piece), picked, 0.0), axis=0, keepdims=True)
-        for part in range(group):
-            t = number * group + part
-            span = slice(t * slots, (t + 1) * slots)
-            w_out[t, 0:nf, :] = weight_ref[0, k, :, span]
-            w_out[t, nf : nf + 1, :] = heights[:, part * slots : (part + 1) * slots]
-
     square = iota((rows, cols), 0) == iota((rows, cols), 1)
 
     def as_row(column):
         return jnp.sum(jnp.where(square, column, 0.0), axis=0, keepdims=True)
-
-    def as_column(row):
-        return jnp.sum(jnp.where(square, row, 0.0), axis=1, keepdims=True)
-
-    flow_out[0] = east_ref[0:1, :]
-    flow_out[1] = east_ref[rows - 1 : rows, :]
-    flow_out[2] = as_row(north_ref[:, 0:1])
-    flow_out[3] = as_row(north_ref[:, cols - 1 : cols])
-
-    pl.semaphore_wait(barrier, devices - 1)
 
     there = (i > 0, i < n_gx - 1, j > 0, j < n_gy - 1, k > 0, k < n_gz - 1)
     who = ((i - 1, j, k), (i + 1, j, k), (i, j - 1, k), (i, j + 1, k), (i, j, k - 1), (i, j, k + 1))
@@ -199,15 +221,6 @@
             device_id=(t // n_gy, t % n_gy, k),
             device_id_type=MESH,
         )
-
-    @pl.loop(0, tiles)
-    def _(t):
-        @pl.when(t != tile)
-        def _():
-            weights_to(t, tile).start()
-
-    start_exchange(flow_out, flow_in, o_send, o_recv, 4)
-    w_in[tile] = w_out[tile]
 
     for ref in (lhs_d, lhs_v, lhs_p, lhs_t, coup, cur, integ):
         ref[...] = jnp.zeros(ref.shape, ref.dtype)
@@ -239,7 +252,7 @@
     total_tl = total_t
     for f in range(4):
         both, once = spots(nf, 2 * faces, f * nfp, faces + f * nfp)
-        p_hi, p_lo = split(proj_ref[f])
+        p_hi, p_lo = split(proj_ref[:, f, :])
         lhs_p[f * nfp : f * nfp + nf, :] = mm(p_hi, both_b)
         lhs_p[faces + f * nfp : faces + f * nfp + nf, :] = mm(p_lo, once_b)
         total_t += mm(mm(eye_b, p_hi, NT).astype(BF16), both)
@@ -265,10 +278,46 @@
             for q in range(nq):
                 value = values[0:nbp, q * ne : (q + 1) * ne]
                 for d in range(3):
-                    term = jac_ref[d, p, q : q + 1, :] * value
+                    term = jac_ref[p, q, d : d + 1, :] * value
                     sums[d] = term if q == 0 else sums[d] + term
             for d in range(3):
                 coup[d * nbp : (d + 1) * nbp, lane] = sums[d]
+
+    def first_sends():
+        for load in loads_in[:3]:
+            load.wait()
+        h_hi, h_lo = split(height_ref[...])
+        for layer in range(n_gz):
+
+            @pl.when(k == layer)
+            def _():
+                for t in range(tiles):
+                    span = slice(t * slots, (t + 1) * slots)
+                    w_out[t, 0:nf, :] = weight_ref[0, :, layer, span]
+
+        for number, piece in enumerate(pieces):
+            hot = ones_where(in_col(k, piece))
+            picked = mm(h_hi, hot) + mm(h_lo, hot)
+            heights = jnp.sum(jnp.where(in_row(k, piece), picked, 0.0), axis=0, keepdims=True)
+            for part in range(group):
+                t = number * group + part
+                w_out[t, nf : nf + 1, :] = heights[:, part * slots : (part + 1) * slots]
+
+        flow_out[0] = east_ref[0:1, :]
+        flow_out[1] = east_ref[rows - 1 : rows, :]
+        flow_out[2] = as_row(north_ref[:, 0:1])
+        flow_out[3] = as_row(north_ref[:, cols - 1 : cols])
+
+        pl.semaphore_wait(barrier, devices - 1)
+
+        @pl.loop(0, tiles)
+        def _(t):
+            @pl.when(t != tile)
+            def _():
+                weights_to(t, tile).start()
+
+        start_exchange(flow_out, flow_in, o_send, o_recv, 4)
+        w_in[tile] = w_out[tile]
 
     weight_now = time_step
     for degree in range(1, 5):
@@ -278,6 +327,8 @@
         if degree < 4:
             cur[...] = moved
         integ[0:nbp, :] += weight_now * moved
+        if degree == 1:
+            first_sends()
 
     traces = halves(lhs_p, integ[...])
     for q in range(nq):
@@ -345,6 +396,7 @@
     couple(integ)
     volume = halves(lhs_v, coup[...])
 
+    loads_in[3].wait()
     @pl.loop(0, nq)
     def _(p):
         lane = pl.ds(pl.multiple_of(p * ne, ne), ne)
@@ -352,7 +404,7 @@
             total = None
             for q in range(nq):
                 own = table[q * nfp : (q + 1) * nfp, f * ne : (f + 1) * ne]
-                term = self_ref[f, q, pl.ds(p, 1), :] * own
+                term = self_ref[q, p, f : f + 1, :] * own
                 total = term if q == 0 else total + term
             numeric[f * nfp : (f + 1) * nfp, lane] = total
 
@@ -366,52 +418,9 @@
             0:nf, f * ne : (f + 1) * ne
         ]
 
-    for f in range(4):
-        face_hot[:, f * ne : (f + 1) * ne] = ones_where(
-            iota((face_hot.shape[0], ne), 0) == source_ref[f : f + 1, :]
-        )
-    hot_own = face_hot[0 : 4 * ne, :]
-    remote = mm(t_hi, hot_own) + mm(t_lo, hot_own)
-    end_exchange(faces_out, faces_in, f_send, f_recv, 6)
-    arrived = jnp.concatenate([faces_in[direction] for direction in range(6)], axis=0)
-    a_hi, a_lo = split(arrived)
-    width = nq * nfp
-    eye_t = ones_where(iota((width, width), 0) == iota((width, width), 1))
-    hot_far = face_hot[4 * ne : 4 * ne + sends, :]
-    remote = remote + mm(mm(eye_t, a_hi, NT).astype(BF16), hot_far)
-    remote = remote + mm(mm(eye_t, a_lo, NT).astype(BF16), hot_far)
-    table[...] = remote
-
-    @pl.loop(0, nq)
-    def _(p):
-        lane = pl.ds(pl.multiple_of(p * ne, ne), ne)
-        for f in range(4):
-            total = numeric[f * nfp : (f + 1) * nfp, lane]
-            for q in range(nq):
-                far = table[q * nfp : (q + 1) * nfp, f * ne : (f + 1) * ne]
-                total = total + other_ref[f, q, pl.ds(p, 1), :] * far
-            numeric[f * nfp : (f + 1) * nfp, lane] = total
-
-    change = volume - halves(lhs_t, numeric[...])
-    finest = mask_ref[...] > 0
-    for q in range(nq):
-        state = state_ref[q]
-        next_ref[q] = jnp.where(finest, state + change[0:nb, q * ne : (q + 1) * ne], state)
-
     end_exchange(flow_out, flow_in, o_send, o_recv, 4)
-    first_row, last_row = iota((rows, cols), 0) == 0, iota((rows, cols), 0) == rows - 1
-    first_col, last_col = iota((rows, cols), 1) == 0, iota((rows, cols), 1) == cols - 1
-
-    def slope_x(grid, rim):
-        before = jnp.where(first_row, rim[0], pltpu.roll(grid, 1, 0))
-        after = jnp.where(last_row, rim[1], pltpu.roll(grid, rows - 1, 0))
-        return (after - before) * 0.5
-
-    def slope_y(grid, rim):
-        before = jnp.where(first_col, as_column(rim[2]), pltpu.roll(grid, 1, 1))
-        after = jnp.where(last_col, as_column(rim[3]), pltpu.roll(grid, cols - 1, 1))
-        return (after - before) * 0.5
-
+    slope_x, slope_y = slopers(rows, cols)
+    loads_in[4].wait()
     slopes = slope_x(east_ref[...], flow_in) + slope_y(north_ref[...], flow_in)
     base = height_ref[...] - ocean_step * (depth_ref[...] * slopes)
 
@@ -438,9 +447,63 @@
     rim_out[3] = as_row(new_height[:, cols - 1 : cols])
     start_exchange(rim_out, rim_in, r_send, r_recv, 4)
     new_height_ref[...] = new_height
+
+    loads_in[5].wait()
+    for f in range(4):
+        face_hot[:, f * ne : (f + 1) * ne] = ones_where(
+            iota((face_hot.shape[0], ne), 0) == source_ref[f : f + 1, :]
+        )
+    hot_own = face_hot[0 : 4 * ne, :]
+    remote = mm(t_hi, hot_own) + mm(t_lo, hot_own)
+    end_exchange(faces_out, faces_in, f_send, f_recv, 6)
+    arrived = jnp.concatenate([faces_in[direction] for direction in range(6)], axis=0)
+    a_hi, a_lo = split(arrived)
+    width = nq * nfp
+    eye_t = ones_where(iota((width, width), 0) == iota((width, width), 1))
+    hot_far = face_hot[4 * ne : 4 * ne + sends, :]
+    remote = remote + mm(mm(eye_t, a_hi, NT).astype(BF16), hot_far)
+    remote = remote + mm(mm(eye_t, a_lo, NT).astype(BF16), hot_far)
+    table[...] = remote
+
+    @pl.loop(0, nq)
+    def _(p):
+        lane = pl.ds(pl.multiple_of(p * ne, ne), ne)
+        for f in range(4):
+            total = numeric[f * nfp : (f + 1) * nfp, lane]
+            for q in range(nq):
+                far = table[q * nfp : (q + 1) * nfp, f * ne : (f + 1) * ne]
+                total = total + other_ref[q, p, f : f + 1, :] * far
+            numeric[f * nfp : (f + 1) * nfp, lane] = total
+
+    change_ref[...] = volume - halves(lhs_t, numeric[...])
     end_exchange(rim_out, rim_in, r_send, r_recv, 4)
-    new_east_ref[...] = east_ref[...] - ocean_step * slope_x(new_height, rim_in)
-    new_north_ref[...] = north_ref[...] - ocean_step * slope_y(new_height, rim_in)
+    rim_ref[...] = rim_in[...]
+
+
+def finish(
+    state_ref,
+    mask_ref,
+    change_ref,
+    height_ref,
+    rim_ref,
+    east_ref,
+    north_ref,
+    next_ref,
+    new_height_ref,
+    new_east_ref,
+    new_north_ref,
+):
+    nq, nb, ne = state_ref.shape
+    finest = mask_ref[...] > 0
+    for q in range(nq):
+        state = state_ref[q]
+        change = change_ref[0:nb, q * ne : (q + 1) * ne]
+        next_ref[q] = jnp.where(finest, state + change, state)
+    slope_x, slope_y = slopers(*height_ref.shape)
+    height = height_ref[...]
+    new_height_ref[...] = height
+    new_east_ref[...] = east_ref[...] - ocean_step * slope_x(height, rim_ref)
+    new_north_ref[...] = north_ref[...] - ocean_step * slope_y(height, rim_ref)
 
 
 def on_device(
@@ -476,17 +539,16 @@
     faces = 4 * nfp
     args = (
         element_state,
-        jacobians,
+        jnp.transpose(jacobians, (1, 2, 0, 3)),
         stiffness,
-        projection,
-        flux_self,
-        flux_other,
+        jnp.transpose(projection, (1, 0, 2)),
+        jnp.transpose(flux_self, (1, 2, 0, 3)),
+        jnp.transpose(flux_other, (1, 2, 0, 3)),
         face_source,
         send_faces,
-        cluster_mask.reshape(1, -1),
         seafloor_face.reshape(1, -1),
         ocean_cell,
-        ocean_weight,
+        jnp.transpose(ocean_weight, (0, 2, 1, 3)),
         height,
         east_flow,
         north_flow,
@@ -518,20 +580,35 @@
     ]
     for count in (tiles, devices, 6, 4, 4):
         scratch += [pltpu.SemaphoreType.DMA((count,)), pltpu.SemaphoreType.DMA((count,))]
+    grid = pltpu.VMEM((rows, cols), F32)
+    flux = pltpu.VMEM((nq, nq, 4, ne), F32)
+    scratch += [flux, flux, grid, grid, grid, grid, pltpu.SemaphoreType.DMA((6,))]
+    vmem, anywhere = pl.BlockSpec(memory_space=pltpu.VMEM), pl.BlockSpec(memory_space=pl.ANY)
+    change, new_height, rim = pl.pallas_call(
+        functools.partial(kernel, (n_gx, n_gy, n_gz, nq, nb, nf, ne, slots, block)),
+        out_shape=(
+            jax.ShapeDtypeStruct((nbp, nq * ne), F32),
+            jax.ShapeDtypeStruct(height.shape, F32),
+            jax.ShapeDtypeStruct((4, 1, cols), F32),
+        ),
+        in_specs=[vmem] * 4 + [anywhere] * 2 + [vmem] * 5 + [anywhere] * 4,
+        out_specs=[vmem] * 3,
+        scratch_shapes=scratch,
+        compiler_params=pltpu.CompilerParams(collective_id=0, has_side_effects=True),
+        name="step",
+    )(*args)
     return pl.pallas_call(
-        functools.partial(kernel, (n_gx, n_gy, n_gz, nq, nb, nf, ne, slots, block)),
+        finish,
         out_shape=(
             jax.ShapeDtypeStruct(element_state.shape, F32),
             jax.ShapeDtypeStruct(height.shape, F32),
             jax.ShapeDtypeStruct(height.shape, F32),
             jax.ShapeDtypeStruct(height.shape, F32),
         ),
-        in_specs=[pl.BlockSpec(memory_space=pltpu.VMEM)] * len(args),
-        out_specs=[pl.BlockSpec(memory_space=pltpu.VMEM)] * 4,
-        scratch_shapes=scratch,
-        compiler_params=pltpu.CompilerParams(collective_id=0, has_side_effects=True),
-        name="step",
-    )(*args)
+        in_specs=[vmem] * 7,
+        out_specs=[vmem] * 4,
+        name="finish",
+    )(element_state, cluster_mask.reshape(1, -1), change, new_height, rim, east_flow, north_flow)
 
 
 def solution(mesh):

time: 36.7 us -> 26.3 us (0.72)
  local copies, waits for them, and re-layouts: 10.1 us -> 0 us
    unnamed x21 -> x0, local copies, waits for them, and re-layouts: 10.1 us -> none
    pallas_call x1, Pallas kernels: 25.6 us -> 23.2 us  [on_device(): pl.pallas_call(functools.partial(kernel, (n_gx, n_gy, n_gz, nq, nb, nf, n...]
    pallas_call x0 -> x1, Pallas kernels: none -> 2.3 us  [on_device(): pl.pallas_call(finish, out_shape=(jax.ShapeDtypeStruct(element_state.shap...]
where the time goes in v1:
time: 26.3 us; the launch traced here: 26.1 us
  Pallas kernels  25.5 us (97%)
  between operations  0.64 us (2%)
    pallas_call x1, Pallas kernels, on_device(): pl.pallas_call(functools.partial(kernel, (n_gx, n_gy, n_gz, nq, nb, nf, n...  23.2 us
    pallas_call x1, Pallas kernels, on_device(): pl.pallas_call(finish, out_shape=(jax.ShapeDtypeStruct(element_state.shap...  2.3 us

profile of v1, /device:TPU:0, one launch (start us, length us, event | category | flops | bytes accessed | tf_op | source)
XLA Modules:
  0.0 26.1 jit_solution(18197743247356799037)
XLA Ops:
  0.6 23.2 %step.1 = (f32[40,1152]{1,0:T(8,128)}, f32[256,256]{1,0:T(8,128)}, f32[4,1,256]{2,1,0:T(1,128)}) custom-call(f32[9,35,128]{2,1,0:T(8,128)} %state_ref.3, f32[9,9,3,128]{3,2,1,0:T(4,128)} %bitcast.8, f32[3,35,35]{2,1,0:T(8,128)} %stiff_ref.1, f32[15,4,35]{2,1,0:T(4,128)} %bitcast.11, f32[9,9,4,128]{3,2,1,0:T(4,128)} %bitcast.9, f32[9,9,4,128]{3,2,1,0:T(4,128)} %bitcast.10, ...), custom_call_target="tpu_custom_call" | custom-call | tf_op jit(solution)/shard_map/step/pallas_call | solution.py:587
  23.8 2.3 %finish.1 = (f32[9,35,128]{2,1,0:T(8,128)}, f32[256,256]{1,0:T(8,128)}, f32[256,256]{1,0:T(8,128)}, f32[256,256]{1,0:T(8,128)}) custom-call(f32[9,35,128]{2,1,0:T(8,128)} %state_ref.3, s32[1,128]{1,0:T(1,128)} %bitcast.13, f32[40,1152]{1,0:T(8,128)} %get-tuple-element.7.change_ref, f32[256,256]{1,0:T(8,128)} %get-tuple-element.8.height_ref, ...), custom_call_target="tpu_custom_call" | custom-call | tf_op jit(solution)/shard_map/finish/pallas_call | solution.py:600

commit v2 on v1

--- a/solution.py
+++ b/solution.py
@@ -27,6 +27,11 @@
 def split(x):
     hi = x.astype(BF16)
     return hi, (x - hi.astype(F32)).astype(BF16)
+
+
+def both(hi, lo, rhs, dims=NN):
+    out = mm(jnp.concatenate([hi, lo], axis=0), rhs, dims)
+    return out[: hi.shape[0]] + out[hi.shape[0] :]
 
 
 def iota(shape, dim):
@@ -126,19 +131,36 @@
     rows, cols = height_ref.shape
     i, j, k = lax.axis_index("gx"), lax.axis_index("gy"), lax.axis_index("gz")
     tile = i * n_gy + j
-    me = tile * n_gz + k
     half = coup.shape[0]
 
-    def place(n):
-        return (n // (n_gy * n_gz), (n // n_gz) % n_gy, n % n_gz)
+    def everyone(act):
+        @pl.loop(0, n_gx)
+        def _(a):
+            @pl.loop(0, n_gy)
+            def _(b):
+                there = a * n_gy + b
+                for c in range(n_gz):
+
+                    @pl.when((there != tile) | (k != c))
+                    def _():
+                        act(a, b, c, there)
+
+    def other_tiles(act):
+        @pl.loop(0, n_gx)
+        def _(a):
+            for b in range(n_gy):
+
+                @pl.when(a * n_gy + b != tile)
+                def _():
+                    act(a, b)
 
     barrier = pltpu.get_barrier_semaphore()
 
-    @pl.loop(0, devices)
-    def _(n):
-        @pl.when(n != me)
-        def _():
-            pl.semaphore_signal(barrier, inc=1, device_id=place(n), device_id_type=MESH)
+    everyone(
+        lambda a, b, c, t: pl.semaphore_signal(
+            barrier, inc=1, device_id=(a, b, c), device_id_type=MESH
+        )
+    )
 
     loads_in = [
         pltpu.make_async_copy(source, target, in_sem.at[number])
@@ -212,13 +234,14 @@
                     device_id_type=MESH,
                 ).wait_recv()
 
-    def weights_to(t, slot):
+    def weights_to(a, b, slot):
+        t = a * n_gy + b
         return pltpu.make_async_remote_copy(
             src_ref=w_out.at[t],
             dst_ref=w_in.at[slot],
             send_sem=w_send.at[t],
             recv_sem=w_recv.at[slot],
-            device_id=(t // n_gy, t % n_gy, k),
+            device_id=(a, b, k),
             device_id_type=MESH,
         )
 
@@ -234,11 +257,11 @@
     total_d = jnp.zeros((nbp, 2 * half), F32)
     total_dl, total_v, total_vl = total_d, total_d, total_d
     for d in range(3):
-        both, once = spots(nb, 2 * half, d * nbp, half + d * nbp)
+        pair, once = spots(nb, 2 * half, d * nbp, half + d * nbp)
         s_hi, s_lo = split(stiff_ref[d])
-        total_d += mm(mm(eye_b, s_hi).astype(BF16), both)
+        total_d += mm(mm(eye_b, s_hi).astype(BF16), pair)
         total_dl += mm(mm(eye_b, s_lo).astype(BF16), once)
-        total_v += mm(mm(eye_b, s_hi, NT).astype(BF16), both)
+        total_v += mm(mm(eye_b, s_hi, NT).astype(BF16), pair)
         total_vl += mm(mm(eye_b, s_lo, NT).astype(BF16), once)
     lhs_d[0:nbp, :] = -total_d
     lhs_d[nbp : 2 * nbp, :] = -total_dl
@@ -251,11 +274,11 @@
     total_t = jnp.zeros((nbp, 2 * faces), F32)
     total_tl = total_t
     for f in range(4):
-        both, once = spots(nf, 2 * faces, f * nfp, faces + f * nfp)
+        pair, once = spots(nf, 2 * faces, f * nfp, faces + f * nfp)
         p_hi, p_lo = split(proj_ref[:, f, :])
         lhs_p[f * nfp : f * nfp + nf, :] = mm(p_hi, both_b)
         lhs_p[faces + f * nfp : faces + f * nfp + nf, :] = mm(p_lo, once_b)
-        total_t += mm(mm(eye_b, p_hi, NT).astype(BF16), both)
+        total_t += mm(mm(eye_b, p_hi, NT).astype(BF16), pair)
         total_tl += mm(mm(eye_b, p_lo, NT).astype(BF16), once)
     lhs_t[0:nbp, :] = total_t
     lhs_t[nbp : 2 * nbp, :] = total_tl
@@ -297,7 +320,7 @@
 
         for number, piece in enumerate(pieces):
             hot = ones_where(in_col(k, piece))
-            picked = mm(h_hi, hot) + mm(h_lo, hot)
+            picked = both(h_hi, h_lo, hot)
             heights = jnp.sum(jnp.where(in_row(k, piece), picked, 0.0), axis=0, keepdims=True)
             for part in range(group):
                 t = number * group + part
@@ -310,11 +333,7 @@
 
         pl.semaphore_wait(barrier, devices - 1)
 
-        @pl.loop(0, tiles)
-        def _(t):
-            @pl.when(t != tile)
-            def _():
-                weights_to(t, tile).start()
+        other_tiles(lambda a, b: weights_to(a, b, tile).start())
 
         start_exchange(flow_out, flow_in, o_send, o_recv, 4)
         w_in[tile] = w_out[tile]
@@ -355,36 +374,28 @@
         floors = floor_ref[:, piece]
         floor_hot[:, piece] = ones_where(iota((4 * ne, floors.shape[1]), 0) == floors)
     vertical = slice((nq - 1) * nfp, nq * nfp)
-    uptrace = mm(t_hi[vertical], floor_hot[...]) + mm(t_lo[vertical], floor_hot[...])
-
-    @pl.loop(0, tiles)
-    def _(t):
-        @pl.when(t != tile)
-        def _():
-            weights_to(t, t).wait()
+    uptrace = both(t_hi[vertical], t_lo[vertical], floor_hot[...])
+
+    other_tiles(lambda a, b: weights_to(a, b, a * n_gy + b).wait())
 
     for t in range(tiles):
         v_out[t] = jnp.sum(
             w_in[t, 0:nf, :] * uptrace[0:nf, t * slots : (t + 1) * slots], axis=0, keepdims=True
         )
 
-    def values_to(n, slot):
+    def values_to(a, b, c, t, slot):
         return pltpu.make_async_remote_copy(
-            src_ref=v_out.at[n // n_gz],
+            src_ref=v_out.at[t],
             dst_ref=v_in.at[slot],
-            send_sem=v_send.at[n],
+            send_sem=v_send.at[c * tiles + t],
             recv_sem=v_recv.at[slot],
-            device_id=place(n),
+            device_id=(a, b, c),
             device_id_type=MESH,
         )
 
     mine = k * tiles + tile
 
-    @pl.loop(0, devices)
-    def _(n):
-        @pl.when(n != me)
-        def _():
-            values_to(n, mine).start()
+    everyone(lambda a, b, c, t: values_to(a, b, c, t, mine).start())
 
     v_in[mine] = v_out[tile]
 
@@ -412,7 +423,7 @@
         [w_in[t] * w_in[t, nf : nf + 1, :] for t in range(tiles)], axis=1
     )
     l_hi, l_lo = split(loads)
-    face_load = mm(l_hi, floor_hot[...], NT) + mm(l_lo, floor_hot[...], NT)
+    face_load = both(l_hi, l_lo, floor_hot[...], NT)
     for f in range(4):
         numeric[f * nfp : f * nfp + nf, 2 * ne : 3 * ne] += face_load[
             0:nf, f * ne : (f + 1) * ne
@@ -424,37 +435,34 @@
     slopes = slope_x(east_ref[...], flow_in) + slope_y(north_ref[...], flow_in)
     base = height_ref[...] - ocean_step * (depth_ref[...] * slopes)
 
-    @pl.loop(0, devices)
-    def _(n):
-        @pl.when(n != me)
-        def _():
-            values_to(n, (n % n_gz) * tiles + n // n_gz).wait()
-
-    source = jnp.zeros((rows, cols), F32)
-    for layer in range(n_gz):
+    everyone(lambda a, b, c, t: values_to(a, b, c, t, c * tiles + t).wait())
+
+    new_height_ref[...] = base
+
+    @pl.loop(0, n_gz)
+    def _(layer):
         for number, piece in enumerate(pieces):
             first = layer * tiles + number * group
             values = jnp.concatenate([v_in[first + part] for part in range(group)], axis=1)
-            v_hi, v_lo = split(values)
-            here, other = in_row(layer, piece), hot_c[layer, :, piece]
-            for part in (v_hi, v_lo):
-                spread = jnp.where(here, part.astype(F32), 0.0).astype(BF16)
-                source += mm(spread, other, NT)
-    new_height = base + ocean_step * source
+            here = in_row(layer, piece)
+            v_hi, v_lo = (
+                jnp.where(here, part.astype(F32), 0.0).astype(BF16) for part in split(values)
+            )
+            new_height_ref[...] += ocean_step * both(v_hi, v_lo, hot_c[layer, :, piece], NT)
+
+    new_height = new_height_ref[...]
     rim_out[0] = new_height[0:1, :]
     rim_out[1] = new_height[rows - 1 : rows, :]
     rim_out[2] = as_row(new_height[:, 0:1])
     rim_out[3] = as_row(new_height[:, cols - 1 : cols])
     start_exchange(rim_out, rim_in, r_send, r_recv, 4)
-    new_height_ref[...] = new_height
-
     loads_in[5].wait()
     for f in range(4):
         face_hot[:, f * ne : (f + 1) * ne] = ones_where(
             iota((face_hot.shape[0], ne), 0) == source_ref[f : f + 1, :]
         )
     hot_own = face_hot[0 : 4 * ne, :]
-    remote = mm(t_hi, hot_own) + mm(t_lo, hot_own)
+    remote = both(t_hi, t_lo, hot_own)
     end_exchange(faces_out, faces_in, f_send, f_recv, 6)
     arrived = jnp.concatenate([faces_in[direction] for direction in range(6)], axis=0)
     a_hi, a_lo = split(arrived)

time: 26.3 us -> 25.8 us (0.981)
  Pallas kernels: 25.5 us -> 25 us
    pallas_call x1, Pallas kernels: 23.2 us -> 22.7 us  [on_device(): pl.pallas_call(functools.partial(kernel, (n_gx, n_gy, n_gz, nq, nb, nf, n...]
where the time goes in v2:
time: 25.8 us; the launch traced here: 25.6 us
  Pallas kernels  25 us (97%)
  between operations  0.64 us (2%)
    pallas_call x1, Pallas kernels, on_device(): pl.pallas_call(functools.partial(kernel, (n_gx, n_gy, n_gz, nq, nb, nf, n...  22.7 us
    pallas_call x1, Pallas kernels, on_device(): pl.pallas_call(finish, out_shape=(jax.ShapeDtypeStruct(element_state.shap...  2.3 us

profile of v2, /device:TPU:0, one launch (start us, length us, event | category | flops | bytes accessed | tf_op | source)
XLA Modules:
  0.0 25.6 jit_solution(15705469703816029447)
XLA Ops:
  0.6 22.7 %step.1 = (f32[40,1152]{1,0:T(8,128)}, f32[256,256]{1,0:T(8,128)}, f32[4,1,256]{2,1,0:T(1,128)}) custom-call(f32[9,35,128]{2,1,0:T(8,128)} %state_ref.3, f32[9,9,3,128]{3,2,1,0:T(4,128)} %bitcast.8, f32[3,35,35]{2,1,0:T(8,128)} %stiff_ref.1, f32[15,4,35]{2,1,0:T(4,128)} %bitcast.11, f32[9,9,4,128]{3,2,1,0:T(4,128)} %bitcast.9, f32[9,9,4,128]{3,2,1,0:T(4,128)} %bitcast.10, ...), custom_call_target="tpu_custom_call" | custom-call | tf_op jit(solution)/shard_map/step/pallas_call | solution.py:595
  23.3 2.3 %finish.1 = (f32[9,35,128]{2,1,0:T(8,128)}, f32[256,256]{1,0:T(8,128)}, f32[256,256]{1,0:T(8,128)}, f32[256,256]{1,0:T(8,128)}) custom-call(f32[9,35,128]{2,1,0:T(8,128)} %state_ref.3, s32[1,128]{1,0:T(1,128)} %bitcast.13, f32[40,1152]{1,0:T(8,128)} %get-tuple-element.7.change_ref, f32[256,256]{1,0:T(8,128)} %get-tuple-element.8.height_ref, ...), custom_call_target="tpu_custom_call" | custom-call | tf_op jit(solution)/shard_map/finish/pallas_call | solution.py:608

commit v3 on v2

--- a/solution.py
+++ b/solution.py
@@ -429,6 +429,13 @@
             0:nf, f * ne : (f + 1) * ne
         ]
 
+    for f in range(4):
+        face_hot[:, f * ne : (f + 1) * ne] = ones_where(
+            iota((face_hot.shape[0], ne), 0) == source_ref[f : f + 1, :]
+        )
+    hot_own = face_hot[0 : 4 * ne, :]
+    table[...] = both(t_hi, t_lo, hot_own)
+
     end_exchange(flow_out, flow_in, o_send, o_recv, 4)
     slope_x, slope_y = slopers(rows, cols)
     loads_in[4].wait()
@@ -457,19 +464,13 @@
     rim_out[3] = as_row(new_height[:, cols - 1 : cols])
     start_exchange(rim_out, rim_in, r_send, r_recv, 4)
     loads_in[5].wait()
-    for f in range(4):
-        face_hot[:, f * ne : (f + 1) * ne] = ones_where(
-            iota((face_hot.shape[0], ne), 0) == source_ref[f : f + 1, :]
-        )
-    hot_own = face_hot[0 : 4 * ne, :]
-    remote = both(t_hi, t_lo, hot_own)
     end_exchange(faces_out, faces_in, f_send, f_recv, 6)
     arrived = jnp.concatenate([faces_in[direction] for direction in range(6)], axis=0)
     a_hi, a_lo = split(arrived)
     width = nq * nfp
     eye_t = ones_where(iota((width, width), 0) == iota((width, width), 1))
     hot_far = face_hot[4 * ne : 4 * ne + sends, :]
-    remote = remote + mm(mm(eye_t, a_hi, NT).astype(BF16), hot_far)
+    remote = table[...] + mm(mm(eye_t, a_hi, NT).astype(BF16), hot_far)
     remote = remote + mm(mm(eye_t, a_lo, NT).astype(BF16), hot_far)
     table[...] = remote
 

time: 25.8 us -> 25.8 us (level)
  no operation moved by 1% of the time
where the time goes in v3:
time: 25.8 us; the launch traced here: 25.6 us
  Pallas kernels  25 us (97%)
  between operations  0.64 us (2%)
    pallas_call x1, Pallas kernels, on_device(): pl.pallas_call(functools.partial(kernel, (n_gx, n_gy, n_gz, nq, nb, nf, n...  22.7 us
    pallas_call x1, Pallas kernels, on_device(): pl.pallas_call(finish, out_shape=(jax.ShapeDtypeStruct(element_state.shap...  2.3 us

profile of v3, /device:TPU:0, one launch (start us, length us, event | category | flops | bytes accessed | tf_op | source)
XLA Modules:
  0.0 25.6 jit_solution(16941736045073171221)
XLA Ops:
  0.6 22.7 %step.1 = (f32[40,1152]{1,0:T(8,128)}, f32[256,256]{1,0:T(8,128)}, f32[4,1,256]{2,1,0:T(1,128)}) custom-call(f32[9,35,128]{2,1,0:T(8,128)} %state_ref.3, f32[9,9,3,128]{3,2,1,0:T(4,128)} %bitcast.8, f32[3,35,35]{2,1,0:T(8,128)} %stiff_ref.1, f32[15,4,35]{2,1,0:T(4,128)} %bitcast.11, f32[9,9,4,128]{3,2,1,0:T(4,128)} %bitcast.9, f32[9,9,4,128]{3,2,1,0:T(4,128)} %bitcast.10, ...), custom_call_target="tpu_custom_call" | custom-call | tf_op jit(solution)/shard_map/step/pallas_call | solution.py:596
  23.3 2.3 %finish.1 = (f32[9,35,128]{2,1,0:T(8,128)}, f32[256,256]{1,0:T(8,128)}, f32[256,256]{1,0:T(8,128)}, f32[256,256]{1,0:T(8,128)}) custom-call(f32[9,35,128]{2,1,0:T(8,128)} %state_ref.3, s32[1,128]{1,0:T(1,128)} %bitcast.13, f32[40,1152]{1,0:T(8,128)} %get-tuple-element.7.change_ref, f32[256,256]{1,0:T(8,128)} %get-tuple-element.8.height_ref, ...), custom_call_target="tpu_custom_call" | custom-call | tf_op jit(solution)/shard_map/finish/pallas_call | solution.py:609
